TPU v7x, 512 devices: a whole 4x4x16 slice. The times are simulated.
512 devices in a mesh: dp: 64 (over x, z), ctx: 8 (over y, core).
Axes of the slice: x: 4, y: 4, z: 16, core: 2. Of those that a mesh axis runs over, the one named last changes fastest.
Arguments:
- projections: bfloat16 [131072, 6144], P(('dp', 'ctx')), may hold values from -6 to 6
- block_source: int32 [64, 8, 2], P('dp', 'ctx'), may hold values from 0 to 1023, as said below
- clip_ids: int32 [64, 16], P('dp'), may hold values from 0 to 8, as said below
- out_weight: bfloat16 [2048, 1536], P('dp'), may hold values from -1 to 1
Outputs:
- mixed: bfloat16 [131072, 1536], P(('dp', 'ctx'))
Inputs may be any that keep to these rules, and one draw needn't show every extreme that they name: `block_source`: arrival block a lies on the device numbered a // 2 in dp-major order (dp index a // (2 * 8), ctx index (a // 2) % 8). The block that fills pack block (o, j, l) lies on the device with the same ctx index j and dp index o or o XOR 1. Every arrival block fills exactly one pack block. `clip_ids`: in each pack the clip numbers start at 0, never fall and rise by at most one from block to block; every clip spans 1 to 8 blocks, and in every pack some clip spans exactly 8 blocks.
All inputs are finite; a program needn't handle non-finite values.
Results may differ from a plain program's by a relative error of at most 0.0057.
Values may be sent and summed in bfloat16 or wider, within the bound.
A program may use at most 64 MiB of HBM per device.

v0:
```python
import math

import jax
import jax.numpy as jnp
from jax import lax
from jax.sharding import PartitionSpec as P

HEAD = 128


big_negative = -1e30


def partner(value, axis, bit):
    mask = 2**bit
    pairs = [(source, source ^ mask) for source in range(lax.axis_size(axis))]
    return lax.ppermute(value, axis, pairs)


def soft_weights(scores, allowed):
    masked = jnp.where(allowed, scores, big_negative)
    row_max = jnp.max(masked, axis=-1, keepdims=True)
    exponent = jnp.exp(masked - row_max)
    return (exponent / jnp.sum(exponent, axis=-1, keepdims=True)).astype(jnp.bfloat16)


def attend_dense(queries, key_rows, value_rows, token_clip, scaling):
    token_count, head_count, head_size = queries.shape
    step_size = min(token_count, 512)
    step_count = token_count // step_size
    query_steps = queries.reshape(step_count, step_size, head_count, head_size)
    clip_steps = token_clip.reshape(step_count, step_size)

    def one_step(arguments):
        query_block, clip_block = arguments
        scores = (
            jnp.einsum("qhe,khe->hqk", query_block, key_rows, preferred_element_type=jnp.float32)
            * scaling
        )
        allowed = (clip_block[:, None] == token_clip[None, :])[None]
        weights = soft_weights(scores, allowed)
        return jnp.einsum(
            "hqk,khe->qhe", weights, value_rows, preferred_element_type=jnp.float32
        ).astype(jnp.bfloat16)

    outputs = lax.map(one_step, (query_steps, clip_steps))
    return outputs.reshape(token_count, head_count, head_size)


def body(projections, block_source, clip_ids, out_weight):
    ctx_count = lax.axis_size("ctx")
    local_rows, row_width = projections.shape
    local_blocks = block_source.shape[2]
    block_rows = local_rows // local_blocks
    own_blocks = projections.reshape(local_blocks, block_rows, row_width)
    partner_blocks = partner(own_blocks, "dp", 0)
    source_ids = block_source.reshape(local_blocks)
    from_partner = source_ids // (local_blocks * ctx_count) != lax.axis_index("dp")
    chosen_slot = source_ids % local_blocks + local_blocks * from_partner.astype(jnp.int32)
    candidates = jnp.concatenate([own_blocks, partner_blocks], axis=0)
    packed = jnp.take(candidates, chosen_slot, axis=0)
    local_heads = row_width // (3 * HEAD) // ctx_count
    grouped = packed.reshape(local_rows, ctx_count, local_heads, 3 * HEAD)
    block_clip = clip_ids.reshape(-1)
    token_clip = jnp.repeat(block_clip, block_rows)
    scaling = 1.0 / math.sqrt(HEAD)
    regrouped = lax.all_to_all(grouped, "ctx", split_axis=1, concat_axis=0, tiled=True)
    token_count = regrouped.shape[0]
    item_count = regrouped.shape[2]
    features = regrouped.reshape(token_count, item_count, 3 * HEAD)
    queries = features[:, :, :HEAD]
    key_rows = features[:, :, HEAD : 2 * HEAD]
    value_rows = features[:, :, 2 * HEAD :]
    attended = attend_dense(queries, key_rows, value_rows, token_clip, scaling)
    merged = attended.reshape(local_rows * ctx_count, local_heads * HEAD)
    attention_rows = lax.all_to_all(merged, "ctx", split_axis=0, concat_axis=1, tiled=True)
    result = jnp.dot(
        attention_rows,
        lax.all_gather(out_weight, "dp", axis=0, tiled=True),
        preferred_element_type=jnp.float32,
    )
    return result.astype(jnp.bfloat16)


def solution(mesh):
    return jax.shard_map(
        body,
        mesh=mesh,
        in_specs=(P(("dp", "ctx"), None), P("dp", "ctx", None), P("dp", None), P("dp", None)),
        out_specs=P(("dp", "ctx"), None),
        check_vma=False,
    )
```

profile of v0, /device:TPU:8, one launch (start us, length us, event | category | flops | bytes accessed | tf_op | source)
XLA Modules:
  0.0 276.1 jit_solution(7214846663131477792)
XLA Ops:
  6.5 3.8 %collective-permute-start = (bf16[2,128,6144]{2,1,0:T(8,128)(2,1)}, bf16[2,128,6144]{2,1,0:T(8,128)(2,1)S(1)}, u32[]{:S(2)}, u32[]{:S(2)}) collective-permute-start(bf16[2,128,6144]{2,1,0:T(8,128)(2,1)} %bitcast.87), channel_id=1, source_target_pairs={{0,8},{8,0},{16,24},{24,16},{32,40},{40,32},{48,56},{56,48},{64,72... | collective-permute-start | bytes 9437192 | tf_op jit(solution)/shard_map/ppermute | solution.py:17
  10.4 0.7 fusion.31
  11.0 0.7 compare_and_fusion
  11.8 66.9 %collective-permute-done = bf16[2,128,6144]{2,1,0:T(8,128)(2,1)S(1)} collective-permute-done((bf16[2,128,6144]{2,1,0:T(8,128)(2,1)}, bf16[2,128,6144]{2,1,0:T(8,128)(2,1)S(1)}, u32[]{:S(2)}, u32[]{:S(2)}) %collective-permute-start) | collective-permute-done | bytes 3145760 | tf_op jit(solution)/shard_map/ppermute | solution.py:17
  78.7 5.1 %pad_maximum_fusion = bf16[4,128,6144]{2,1,0:T(8,128)(2,1)} fusion(bf16[2,128,6144]{2,1,0:T(8,128)(2,1)S(1)} %collective-permute-done, bf16[2,128,6144]{2,1,0:T(8,128)(2,1)} %bitcast.88), kind=kLoop, calls=%fused_computation.27 | loop fusion | flops 3145728 | bytes 12582912 | tf_op jit(solution)/shard_map/concatenate | solution.py:60
  83.7 3.5 %gather_fusion = bf16[2,128,6144]{2,1,0:T(8,128)(2,1)S(1)} fusion(bf16[4,128,6144]{2,1,0:T(8,128)(2,1)} %pad_maximum_fusion, s32[1024]{0:T(1024)S(1)} %pad_clamp_fusion), kind=kCustom, calls=%fused_computation | custom fusion | bytes 6291464 | tf_op jit(solution)/shard_map/jit(_take)/gather | solution.py:61
  87.3 3.5 %gather.7 = bf16[256,8,2,384]{3,2,1,0:T(2,128)(2,1)} reshape(bf16[2,128,6144]{2,1,0:T(8,128)(2,1)S(1)} %gather_fusion) | data formatting | bytes 6291456 | tf_op jit(solution)/shard_map/jit(_take)/gather | solution.py:61
  90.8 5.0 %broadcast_select_fusion = bf16[256,8,2,384]{3,2,1,0:T(2,128)(2,1)S(1)} fusion(bf16[256,8,2,384]{3,2,1,0:T(2,128)(2,1)} %gather.7, pred[256]{0:T(512)(128)(4,1)S(1)} %broadcast_bitcast_fusion.2), kind=kLoop, calls=%fused_computation.28 | loop fusion | flops 1572864 | bytes 6291712 | tf_op jit(solution)/shard_map/jit(_take)/select_n | solution.py:61
  95.8 4.1 %copy.12 = bf16[256,8,2,384]{3,2,0,1:T(2,128)(2,1)} copy(bf16[256,8,2,384]{3,2,1,0:T(2,128)(2,1)S(1)} %broadcast_select_fusion) | data formatting | bytes 6291456 | tf_op jit(solution)/shard_map/jit(_take)/select_n | solution.py:61
  99.9 5.0 %all-to-all-start = ((bf16[256,8,2,384]{3,2,0,1:T(2,128)(2,1)}), bf16[256,8,2,384]{3,2,0,1:T(2,128)(2,1)S(1)}, u32[]{:S(2)}, u32[]{:S(2)}) async-start(bf16[256,8,2,384]{3,2,0,1:T(2,128)(2,1)} %copy.12), calls=%async_computation | async-start | bytes 6291456 | tf_op jit(solution)/shard_map/all_to_all | solution.py:67
  104.9 0.7 all-gather.2.cloned.1.call-update
  106.1 0.6 reduce.3
  106.9 35.0 %all-to-all-done = bf16[256,8,2,384]{3,2,0,1:T(2,128)(2,1)S(1)} async-done(((bf16[256,8,2,384]{3,2,0,1:T(2,128)(2,1)}), bf16[256,8,2,384]{3,2,0,1:T(2,128)(2,1)S(1)}, u32[]{:S(2)}, u32[]{:S(2)}) %all-to-all-start) | async-done | bytes 3145760 | tf_op jit(solution)/shard_map/all_to_all | solution.py:67
  141.9 0.6 copy.13
  142.5 1.9 fusion.37
  144.3 53.7 %while.11 = (s32[]{:T(128)}, bf16[4,512,2,128]{3,2,1,0:T(2,128)(2,1)S(1)}, s32[4,512]{1,0:T(4,128)S(1)}, bf16[4,512,2,128]{3,1,0,2:T(8,128)(2,1)}, bf16[2048,2,1...) while((s32[]{:T(128)}, ...), condition=%wide.region_3.4_spmd.clone, body=%wide.region_0.3_spmd.clone.sunk | while | flops 1087506432 | bytes 22051484 | solution.py:46
  144.4 0.7 broadcast_compare_fusion.2
  145.1 7.7 %fusion.51 = (f32[2,512]{1,0:T(2,128)S(1)}, f32[2,512,2048]{2,1,0:T(8,128)}) fusion(pred[512,2048]{1,0:T(8,128)(4,1)S(1)} %broadcast_compare_fusion.2, bf16[2048,2,128]{2,0,1:T(8,128)(2,1)} %get-tuple-element.167, bf16[4,512,2,128]{3,1,0,2:T(8,128)(2,1)} %get-tuple-element.166, s32[]{:T(128)} %get-tuple-element.155), kind=kOutput, calls=%fused_computation.56.clone.1 | convolution fusion | flops 545261568 | bytes 10752512 | tf_op jit(solution)/shard_map/while/body/eval_jaxpr/sub | solution.py:23
  152.7 4.7 %fusion.52 = bf16[1,512,2,128]{3,1,2,0:T(8,128)(2,1)S(1)} fusion(bf16[2048,2,128]{2,0,1:T(8,128)(2,1)S(1)} %get-tuple-element.168, f32[2,512,2048]{2,1,0:T(8,128)} %get-tuple-element.145, f32[2,512]{1,0:T(2,128)S(1)} %get-tuple-element.146), kind=kOutput, calls=%fused_computation.13.clone.1 | convolution fusion | flops 541196288 | bytes 9703424 | tf_op jit(solution)/shard_map/while/body/eval_jaxpr/hqk,khe->qhe/dot_general | solution.py:42
  157.8 0.7 broadcast_compare_fusion.2
  158.5 7.7 %fusion.51 = (f32[2,512]{1,0:T(2,128)S(1)}, f32[2,512,2048]{2,1,0:T(8,128)}) fusion(pred[512,2048]{1,0:T(8,128)(4,1)S(1)} %broadcast_compare_fusion.2, bf16[2048,2,128]{2,0,1:T(8,128)(2,1)} %get-tuple-element.167, bf16[4,512,2,128]{3,1,0,2:T(8,128)(2,1)} %get-tuple-element.166, s32[]{:T(128)} %get-tuple-element.155), kind=kOutput, calls=%fused_computation.56.clone.1 | convolution fusion | flops 545261568 | bytes 10752512 | tf_op jit(solution)/shard_map/while/body/eval_jaxpr/sub | solution.py:23
  166.2 4.7 %fusion.52 = bf16[1,512,2,128]{3,1,2,0:T(8,128)(2,1)S(1)} fusion(bf16[2048,2,128]{2,0,1:T(8,128)(2,1)S(1)} %get-tuple-element.168, f32[2,512,2048]{2,1,0:T(8,128)} %get-tuple-element.145, f32[2,512]{1,0:T(2,128)S(1)} %get-tuple-element.146), kind=kOutput, calls=%fused_computation.13.clone.1 | convolution fusion | flops 541196288 | bytes 9703424 | tf_op jit(solution)/shard_map/while/body/eval_jaxpr/hqk,khe->qhe/dot_general | solution.py:42
  171.3 0.7 broadcast_compare_fusion.2
  171.9 7.7 %fusion.51 = (f32[2,512]{1,0:T(2,128)S(1)}, f32[2,512,2048]{2,1,0:T(8,128)}) fusion(pred[512,2048]{1,0:T(8,128)(4,1)S(1)} %broadcast_compare_fusion.2, bf16[2048,2,128]{2,0,1:T(8,128)(2,1)} %get-tuple-element.167, bf16[4,512,2,128]{3,1,0,2:T(8,128)(2,1)} %get-tuple-element.166, s32[]{:T(128)} %get-tuple-element.155), kind=kOutput, calls=%fused_computation.56.clone.1 | convolution fusion | flops 545261568 | bytes 10752512 | tf_op jit(solution)/shard_map/while/body/eval_jaxpr/sub | solution.py:23
  179.6 4.7 %fusion.52 = bf16[1,512,2,128]{3,1,2,0:T(8,128)(2,1)S(1)} fusion(bf16[2048,2,128]{2,0,1:T(8,128)(2,1)S(1)} %get-tuple-element.168, f32[2,512,2048]{2,1,0:T(8,128)} %get-tuple-element.145, f32[2,512]{1,0:T(2,128)S(1)} %get-tuple-element.146), kind=kOutput, calls=%fused_computation.13.clone.1 | convolution fusion | flops 541196288 | bytes 9703424 | tf_op jit(solution)/shard_map/while/body/eval_jaxpr/hqk,khe->qhe/dot_general | solution.py:42
  184.7 0.7 broadcast_compare_fusion.2
  185.3 7.7 %fusion.51 = (f32[2,512]{1,0:T(2,128)S(1)}, f32[2,512,2048]{2,1,0:T(8,128)}) fusion(pred[512,2048]{1,0:T(8,128)(4,1)S(1)} %broadcast_compare_fusion.2, bf16[2048,2,128]{2,0,1:T(8,128)(2,1)} %get-tuple-element.167, bf16[4,512,2,128]{3,1,0,2:T(8,128)(2,1)} %get-tuple-element.166, s32[]{:T(128)} %get-tuple-element.155), kind=kOutput, calls=%fused_computation.56.clone.1 | convolution fusion | flops 545261568 | bytes 10752512 | tf_op jit(solution)/shard_map/while/body/eval_jaxpr/sub | solution.py:23
  193.0 4.7 %fusion.52 = bf16[1,512,2,128]{3,1,2,0:T(8,128)(2,1)S(1)} fusion(bf16[2048,2,128]{2,0,1:T(8,128)(2,1)S(1)} %get-tuple-element.168, f32[2,512,2048]{2,1,0:T(8,128)} %get-tuple-element.145, f32[2,512]{1,0:T(2,128)S(1)} %get-tuple-element.146), kind=kOutput, calls=%fused_computation.13.clone.1 | convolution fusion | flops 541196288 | bytes 9703424 | tf_op jit(solution)/shard_map/while/body/eval_jaxpr/hqk,khe->qhe/dot_general | solution.py:42
  198.0 0.7 all_to_all.28
  198.7 18.5 %all_to_all.34 = bf16[8,256,256]{2,1,0:T(8,128)(2,1)S(1)} all-to-all(bf16[8,256,256]{2,1,0:T(8,128)(2,1)S(1)} %all_to_all.28), channel_id=1, replica_groups=mesh['dp'=64,'ctx'=8] {'ctx'}, dimensions={0} | all-to-all | bytes 2097152 | tf_op jit(solution)/shard_map/all_to_all | solution.py:76
  217.7 46.0 %all-gather.2.cloned.1.call-done = bf16[2048,1536]{1,0:T(8,128)(2,1)} async-done(((bf16[32,1536]{1,0:T(8,128)(2,1)}), bf16[2048,1536]{1,0:T(8,128)(2,1)}) %all-gather.2.cloned.1.call-update) | async-done | bytes 6291472 | tf_op jit(solution)/shard_map/all_gather | solution.py:79
  263.7 5.5 %convolution_convert_fusion = bf16[256,1536]{1,0:T(8,128)(2,1)} fusion(bf16[256,2048]{0,1:T(8,128)(2,1)S(1)} %bitcast.85, bf16[2048,1536]{1,0:T(8,128)(2,1)} %all-gather.2.cloned.1.call-done), kind=kOutput, calls=%fused_computation.29 | convolution fusion | flops 1611005952 | bytes 8126464 | tf_op jit(solution)/shard_map/dot_general | solution.py:77
  (25 shorter events, 2.8 us)
Async XLA Ops:
  6.5 72.1 %collective-permute-start = (bf16[2,128,6144]{2,1,0:T(8,128)(2,1)}, bf16[2,128,6144]{2,1,0:T(8,128)(2,1)S(1)}, u32[]{:S(2)}, u32[]{:S(2)}) collective-permute-start(bf16[2,128,6144]{2,1,0:T(8,128)(2,1)} %bitcast.87), channel_id=1, source_target_pairs={{0,8},{8,0},{16,24},{24,16},{32,40},{40,32},{48,56},{56,48},{64,72... | collective-permute-start | bytes 9437192 | tf_op jit(solution)/shard_map/ppermute | solution.py:17
  99.9 6.3 %copy-start.1 = (s32[1,16]{1,0:T(1,128)S(1)}, s32[1,16]{1,0:T(1,128)}, u32[]{:S(2)}) copy-start(s32[1,16]{1,0:T(1,128)} %param.8) | copy-start | bytes 196
  99.9 42.0 %all-to-all-start = ((bf16[256,8,2,384]{3,2,0,1:T(2,128)(2,1)}), bf16[256,8,2,384]{3,2,0,1:T(2,128)(2,1)S(1)}, u32[]{:S(2)}, u32[]{:S(2)}) async-start(bf16[256,8,2,384]{3,2,0,1:T(2,128)(2,1)} %copy.12), calls=%async_computation | async-start | bytes 6291456 | tf_op jit(solution)/shard_map/all_to_all | solution.py:67
  104.9 158.8 %all-gather.2.cloned.1.call-start = ((), (), s32[]{:S(2)}) async-start(), calls=%async_computation.2 | async-start | bytes 6389760 | tf_op jit(solution)/shard_map/all_gather | solution.py:79
  142.4 1.9 copy-start
Sparse Core Ops, SparseCore 0:
  108.7 155.0 all-gather.1
where the time goes:
time: 277 us; the launch traced here: 276 us
  waiting for transfers between devices  149 us (54%)
  matrix products  54.9 us (20%)
  blocking collectives  18.5 us (7%)
  local copies, waits for them, and re-layouts  17.1 us (6%)
  other arithmetic  14.6 us (5%)
  between operations  13.5 us (5%)
  starting transfers between devices  8.87 us (3%)
    ppermute x1, waiting for transfers between devices, partner(): return lax.ppermute(value, axis, pairs)  66.9 us
    all_gather x1, waiting for transfers between devices, body(): lax.all_gather(out_weight, 'dp', axis=0, tiled=True)  46 us
    all_to_all x1, waiting for transfers between devices, body(): lax.all_to_all(grouped, 'ctx', split_axis=1, concat_axis=0, tiled=True)  35 us
    sub x4, matrix products, soft_weights(): exponent = jnp.exp(masked - row_max)  30.7 us
    dot_general x4, matrix products, one_step(): jnp.einsum('hqk,khe->qhe', weights, value_rows, preferred_element_type=jn...  18.7 us
    all_to_all x1, blocking collectives, body(): lax.all_to_all(merged, 'ctx', split_axis=0, concat_axis=1, tiled=True)  18.5 us
    gather x2, local copies, waits for them, and re-layouts, body(): packed = jnp.take(candidates, chosen_slot, axis=0)  7.07 us
    select_n x2, other arithmetic, body(): packed = jnp.take(candidates, chosen_slot, axis=0)  5.63 us
  transfers between devices with their start and end apart: 3, of which 3 were waited for; matrix products, arithmetic and copies ran while one was open for 21% of the time, Pallas kernels for 0%

commit v1 on v0

v1 whole, which is shorter than its diff:
```python
import functools
import math

import jax
import jax.numpy as jnp
from jax import lax
from jax.experimental import pallas as pl
from jax.experimental.pallas import tpu as pltpu
from jax.sharding import PartitionSpec as P

HEAD = 128
BLK = 128
PACK = 16
WIN = 8
GROUP = 16
MESH = pl.DeviceIdType.MESH
NEG = -1e30
EXP2_SCALE = math.log2(math.e) / math.sqrt(HEAD)
PEERS = [
    (1, 0, 0), (0, 1, 0), (0, 3, 0), (1, 1, 0), (0, 2, 0), (1, 3, 0), (0, 1, 1), (1, 2, 0),
    (0, 3, 1), (1, 0, 1), (0, 2, 1), (1, 1, 1), (1, 3, 1), (1, 2, 1), (0, 0, 1),
]


def place(ds, dy, dc):
    dp = lax.axis_index("dp")
    ctx = lax.axis_index("ctx")
    side = dp % 2
    to_side = (side + ds) % 2
    to_ctx = ((ctx // 2 + dy) % 4) * 2 + (ctx % 2 + dc) % 2
    return (dp - side + to_side, to_ctx), to_side * 8 + to_ctx


def kernel(
    meta_ref, proj_ref, out_ref,
    q_recv, k_recv, v_recv, meta_recv, meta_smem, k_pack, v_pack, probs, sent, merged,
    send_sem, recv_sem, meta_send, meta_sem, out_send, out_sem, local_sem,
):
    recv = (q_recv, k_recv, v_recv)
    me = (lax.axis_index("dp") % 2) * 8 + lax.axis_index("ctx")

    def columns(rank, kind):
        return pl.ds(pl.multiple_of(rank * (3 * HEAD) + kind * HEAD, HEAD), HEAD)

    own = []
    for kind in range(3):
        own.append(
            pltpu.make_async_copy(
                proj_ref.at[:, :, columns(me, kind)], recv[kind].at[pl.ds(2 * me, 2)], local_sem.at[kind]
            )
        )
    own.append(pltpu.make_async_copy(meta_ref, meta_recv.at[me], local_sem.at[3]))
    for copy in own:
        copy.start()

    barrier = pltpu.get_barrier_semaphore()
    for peer in PEERS:
        device, _ = place(*peer)
        pl.semaphore_signal(barrier, inc=1, device_id=device, device_id_type=MESH)
    pl.semaphore_wait(barrier, len(PEERS))

    started = []
    for i, peer in enumerate(PEERS):
        device, rank = place(*peer)
        started.append(
            pltpu.make_async_remote_copy(
                src_ref=meta_ref, dst_ref=meta_recv.at[me], send_sem=meta_send.at[i],
                recv_sem=meta_sem.at[me], device_id=device, device_id_type=MESH,
            )
        )
        started[-1].start()
    for kind in (1, 0, 2):
        for i, peer in enumerate(PEERS):
            device, rank = place(*peer)
            started.append(
                pltpu.make_async_remote_copy(
                    src_ref=proj_ref.at[:, :, columns(rank, kind)], dst_ref=recv[kind].at[pl.ds(2 * me, 2)],
                    send_sem=send_sem.at[kind, i], recv_sem=recv_sem.at[kind, me],
                    device_id=device, device_id_type=MESH,
                )
            )
            started[-1].start()

    def wait_kind(kind):
        for i, peer in enumerate(PEERS):
            device, rank = place(*peer)
            pltpu.make_async_remote_copy(
                src_ref=recv[kind].at[pl.ds(2 * rank, 2)], dst_ref=recv[kind].at[pl.ds(2 * rank, 2)],
                send_sem=send_sem.at[kind, i], recv_sem=recv_sem.at[kind, rank],
                device_id=device, device_id_type=MESH,
            ).wait_recv()
        own[kind].wait()

    for i, peer in enumerate(PEERS):
        device, rank = place(*peer)
        pltpu.make_async_remote_copy(
            src_ref=meta_recv.at[rank], dst_ref=meta_recv.at[rank], send_sem=meta_send.at[i],
            recv_sem=meta_sem.at[rank], device_id=device, device_id_type=MESH,
        ).wait_recv()
    own[3].wait()
    to_smem = pltpu.make_async_copy(meta_recv, meta_smem, local_sem.at[4])
    to_smem.start()
    to_smem.wait()

    def source(pack, block):
        return meta_smem[pack * 8 + block // 2, 0, block % 2]

    def clip(pack, block):
        return meta_smem[pack * 8, 0, 2 + block]

    def window(pack, block):
        first = block
        for back in range(1, WIN):
            at = jnp.maximum(block - back, 0)
            first = jnp.where(clip(pack, at) == clip(pack, block), jnp.minimum(first, at), first)
        return jnp.minimum(first, PACK - WIN)

    def gather(kind, target):
        def step(i, carry):
            target[i, :, pl.ds(0, HEAD)] = recv[kind][source(i // PACK, i % PACK)]
            return carry

        lax.fori_loop(0, 2 * PACK, step, 0)

    v_pack[:, :, HEAD:] = jnp.ones((2 * PACK, BLK, HEAD), jnp.bfloat16)
    wait_kind(1)
    gather(1, k_pack)
    wait_kind(0)

    def score_step(i, carry):
        pack, block = i // PACK, i % PACK
        start = window(pack, block)
        queries = q_recv[source(pack, block)]
        keys = k_pack[pl.ds(pack * PACK + start, WIN)].reshape(WIN * BLK, HEAD)
        scores = lax.dot_general(queries, keys, (((1,), (1,)), ((), ())), preferred_element_type=jnp.float32)
        parts = []
        for w in range(WIN):
            bias = jnp.where(clip(pack, start + w) == clip(pack, block), 0.0, NEG)
            parts.append(scores[:, w * BLK : (w + 1) * BLK] + bias)
        top = functools.reduce(jnp.maximum, parts)
        row_max = jnp.max(top, axis=1, keepdims=True)
        for w in range(WIN):
            probs[i, :, w * BLK : (w + 1) * BLK] = jnp.exp2((parts[w] - row_max) * EXP2_SCALE).astype(jnp.bfloat16)
        return carry

    lax.fori_loop(0, 2 * PACK, score_step, 0)
    wait_kind(2)
    gather(2, v_pack)

    def attend(rank):
        pack = rank // 8
        for slot in range(2):
            block = (rank % 8) * 2 + slot
            i = pack * PACK + block
            values = v_pack[pl.ds(pack * PACK + window(pack, block), WIN)].reshape(WIN * BLK, 2 * HEAD)
            total = jnp.dot(probs[i], values, preferred_element_type=jnp.float32)
            sent[rank, slot] = (total[:, :HEAD] / total[:, HEAD:]).astype(jnp.bfloat16)

    def my_columns(rank):
        return pl.ds(pl.multiple_of(rank * HEAD, HEAD), HEAD)

    def send_step(k, carry):
        ds, dy, dc = k % 2, (k // 2) % 4, k // 8
        device, rank = place(ds, dy, dc)
        attend(rank)
        pltpu.make_async_remote_copy(
            src_ref=sent.at[rank], dst_ref=merged.at[:, :, my_columns(me)], send_sem=out_send.at[k],
            recv_sem=out_sem.at[me], device_id=device, device_id_type=MESH,
        ).start()
        return carry

    lax.fori_loop(1, GROUP, send_step, 0)
    attend(me)
    keep = pltpu.make_async_copy(sent.at[me], merged.at[:, :, my_columns(me)], local_sem.at[3])
    keep.start()
    keep.wait()
    for k in range(1, GROUP):
        device, rank = place(k % 2, (k // 2) % 4, k // 8)
        copy = pltpu.make_async_remote_copy(
            src_ref=sent.at[rank], dst_ref=merged.at[:, :, my_columns(rank)], send_sem=out_send.at[k],
            recv_sem=out_sem.at[rank], device_id=device, device_id_type=MESH,
        )
        copy.wait_send()
        copy.wait_recv()
    for copy in started:
        copy.wait_send()
    finish = pltpu.make_async_copy(merged, out_ref, local_sem.at[4])
    finish.start()
    finish.wait()


def body(projections, block_source, clip_ids, out_weight):
    rows, width = projections.shape
    heads = width // (3 * HEAD)
    meta = jnp.concatenate([block_source.reshape(-1) % (2 * PACK), clip_ids.reshape(-1)])
    meta = jnp.pad(meta[None, :], ((0, 7), (0, 128 - meta.shape[0])))
    kinds = pltpu.SemaphoreType.DMA((3, GROUP))
    ranks = pltpu.SemaphoreType.DMA((GROUP,))
    attended = pl.pallas_call(
        kernel,
        out_shape=jax.ShapeDtypeStruct((2, BLK, heads * HEAD), jnp.bfloat16),
        in_specs=[pl.BlockSpec(memory_space=pl.ANY)] * 2,
        out_specs=pl.BlockSpec(memory_space=pl.ANY),
        scratch_shapes=[
            pltpu.VMEM((2 * PACK, BLK, HEAD), jnp.bfloat16),
            pltpu.VMEM((2 * PACK, BLK, HEAD), jnp.bfloat16),
            pltpu.VMEM((2 * PACK, BLK, HEAD), jnp.bfloat16),
            pltpu.VMEM((GROUP, 8, 128), jnp.int32),
            pltpu.SMEM((GROUP, 8, 128), jnp.int32),
            pltpu.VMEM((2 * PACK, BLK, HEAD), jnp.bfloat16),
            pltpu.VMEM((2 * PACK, BLK, 2 * HEAD), jnp.bfloat16),
            pltpu.VMEM((2 * PACK, BLK, WIN * BLK), jnp.bfloat16),
            pltpu.VMEM((GROUP, 2, BLK, HEAD), jnp.bfloat16),
            pltpu.VMEM((2, BLK, heads * HEAD), jnp.bfloat16),
            kinds, kinds, ranks, ranks, ranks, ranks,
            pltpu.SemaphoreType.DMA((5,)),
        ],
        compiler_params=pltpu.CompilerParams(
            collective_id=0, has_side_effects=True, vmem_limit_bytes=48 * 2**20
        ),
        name="attend",
    )(meta, projections.reshape(2, BLK, width))
    result = jnp.dot(
        attended.reshape(rows, heads * HEAD),
        lax.all_gather(out_weight, "dp", axis=0, tiled=True),
        preferred_element_type=jnp.float32,
    )
    return result.astype(jnp.bfloat16)


def solution(mesh):
    return jax.shard_map(
        body,
        mesh=mesh,
        in_specs=(P(("dp", "ctx"), None), P("dp", "ctx", None), P("dp", None), P("dp", None)),
        out_specs=P(("dp", "ctx"), None),
        check_vma=False,
    )
```

time: 277 us -> 178 us (0.64)
  the two profiles are of different devices: /device:TPU:8 before, /device:TPU:32 now
where the time goes in v1:
time: 178 us
  waiting for transfers between devices  88.2 us (50%)
  Pallas kernels  67.5 us (38%)
  between operations  13.4 us (8%)
  matrix products  5.45 us (3%)
  local copies, waits for them, and re-layouts  1.9 us (1%)
    all_gather x1, waiting for transfers between devices, body(): lax.all_gather(out_weight, 'dp', axis=0, tiled=True)  87.5 us
    pallas_call x1, Pallas kernels, body(): pl.pallas_call(kernel, out_shape=jax.ShapeDtypeStruct((2, BLK, heads * HE...  67.5 us
    dot_general x1, matrix products, body(): jnp.dot(attended.reshape(rows, heads * HEAD), lax.all_gather(out_weight,...  5.45 us
  transfers between devices with their start and end apart: 1, of which 1 were waited for; matrix products, arithmetic and copies ran while one was open for 1% of the time, Pallas kernels for 38%

profile of v1, /device:TPU:32, one launch (start us, length us, event | category | flops | bytes accessed | tf_op | source)
XLA Modules:
  0.0 177.9 jit_solution(8359214596922630953)
XLA Ops:
  6.5 0.0 all-gather.2.cloned.1.call-start
  6.5 0.7 all-gather.2.cloned.1.call-update
  7.3 0.7 and_select_fusion
  7.9 0.7 add_bitcast_fusion
  8.7 0.0 copy-start
  8.7 1.9 %copy-done = bf16[256,6144]{1,0:T(8,128)(2,1)S(1)} copy-done((bf16[256,6144]{1,0:T(8,128)(2,1)S(1)}, bf16[256,6144]{1,0:T(8,128)(2,1)}, u32[]{:S(2)}) %copy-start) | copy-done | bytes 3145752
  10.5 67.5 %attend.1 = bf16[2,128,2048]{2,1,0:T(8,128)(2,1)S(1)} custom-call(s32[8,128]{1,0:T(8,128)S(1)} %pad.4.meta_ref, bf16[2,128,6144]{2,1,0:T(8,128)(2,1)S(1)} %bitcast.9), custom_call_target="tpu_custom_call" | custom-call | tf_op jit(solution)/shard_map/attend/pallas_call | solution.py:199
  78.1 87.5 %all-gather.2.cloned.1.call-done = bf16[2048,1536]{1,0:T(8,128)(2,1)} async-done(((bf16[32,1536]{1,0:T(8,128)(2,1)}), bf16[2048,1536]{1,0:T(8,128)(2,1)}) %all-gather.2.cloned.1.call-update) | async-done | bytes 6291472 | tf_op jit(solution)/shard_map/all_gather | solution.py:225
  165.6 5.5 %convolution_convert_fusion = bf16[256,1536]{1,0:T(8,128)(2,1)} fusion(bf16[256,2048]{1,0:T(8,128)(2,1)S(1)} %bitcast.10, bf16[2048,1536]{1,0:T(8,128)(2,1)} %all-gather.2.cloned.1.call-done), kind=kOutput, calls=%fused_computation | convolution fusion | flops 1611005952 | bytes 8126464 | tf_op jit(solution)/shard_map/dot_general | solution.py:223
  (1 shorter events, 0.0 us)
Async XLA Ops:
  6.5 159.0 %all-gather.2.cloned.1.call-start = ((), (), s32[]{:S(2)}) async-start(), calls=%async_computation | async-start | bytes 6389760 | tf_op jit(solution)/shard_map/all_gather | solution.py:225
  8.7 1.9 %copy-start = (bf16[256,6144]{1,0:T(8,128)(2,1)S(1)}, bf16[256,6144]{1,0:T(8,128)(2,1)}, u32[]{:S(2)}) copy-start(bf16[256,6144]{1,0:T(8,128)(2,1)} %param.4) | copy-start | bytes 9437188
Sparse Core Ops, SparseCore 0:
  10.3 155.2 all-gather.1

commit v2 on v1

--- a/solution.py
+++ b/solution.py
@@ -14,6 +14,9 @@
 WIN = 8
 GROUP = 16
 MESH = pl.DeviceIdType.MESH
+N_X, N_Z = 4, 16
+TILE = 256
+FIRST, BATCH, EARLY = 10, 7, 5
 NEG = -1e30
 EXP2_SCALE = math.log2(math.e) / math.sqrt(HEAD)
 PEERS = [
@@ -32,15 +35,25 @@
 
 
 def kernel(
-    meta_ref, proj_ref, out_ref,
-    q_recv, k_recv, v_recv, meta_recv, meta_smem, k_pack, v_pack, probs, sent, merged,
-    send_sem, recv_sem, meta_send, meta_sem, out_send, out_sem, local_sem,
+    meta_ref, proj_ref, w_ref, out_ref,
+    q_recv, k_recv, v_recv, meta_recv, meta_smem, k_pack, v_pack, probs, sent, merged, w_all, tiles,
+    send_sem, recv_sem, meta_send, meta_sem, out_send, out_sem, w_sem, w_sends, local_sem,
 ):
     recv = (q_recv, k_recv, v_recv)
     me = (lax.axis_index("dp") % 2) * 8 + lax.axis_index("ctx")
 
     def columns(rank, kind):
         return pl.ds(pl.multiple_of(rank * (3 * HEAD) + kind * HEAD, HEAD), HEAD)
+
+    dp = lax.axis_index("dp")
+    ctx = lax.axis_index("ctx")
+    x, z, core = dp // N_Z, dp % N_Z, ctx % 2
+    shard, features = w_ref.shape
+    half = pl.ds(pl.multiple_of(core * (features // 2), HEAD), features // 2)
+    sibling = (dp, ctx - core + (core + 1) % 2)
+    right = (x * N_Z + (z + 1) % N_Z, ctx)
+    left = (x * N_Z + (z + N_Z - 1) % N_Z, ctx)
+    across = [(((x + dx) % N_X) * N_Z + z, ctx) for dx in range(1, N_X)]
 
     own = []
     for kind in range(3):
@@ -50,28 +63,62 @@
             )
         )
     own.append(pltpu.make_async_copy(meta_ref, meta_recv.at[me], local_sem.at[3]))
+    own.append(pltpu.make_async_copy(w_ref, w_all.at[dp], local_sem.at[5]))
     for copy in own:
         copy.start()
 
     barrier = pltpu.get_barrier_semaphore()
-    for peer in PEERS:
-        device, _ = place(*peer)
+    greet = [place(*peer)[0] for peer in PEERS] + across
+    greet.append((x * N_Z + (z + N_Z - 1 + 2 * (z % 2)) % N_Z, ctx))
+    for device in greet:
         pl.semaphore_signal(barrier, inc=1, device_id=device, device_id_type=MESH)
-    pl.semaphore_wait(barrier, len(PEERS))
+    pl.semaphore_wait(barrier, len(greet))
+
+    def chunk(dx, dz):
+        return ((x + dx) % N_X) * N_Z + (z + N_Z + dz) % N_Z
+
+    def weight_copy(at, device, sender, first=False, sem=None):
+        return pltpu.make_async_remote_copy(
+            src_ref=w_ref.at[:, half] if first else w_all.at[at, :, half], dst_ref=w_all.at[at, :, half],
+            send_sem=w_sends.at[sender], recv_sem=w_sem.at[at] if sem is None else sem,
+            device_id=device, device_id_type=MESH,
+        )
+
+    def hand_over(at):
+        weight_copy(at, sibling, 0, sem=w_sem.at[N_X * N_Z]).start()
+
+    def spread(at, first=False):
+        for i in range(N_X - 1):
+            weight_copy(at, across[i], 1 + i, first).start()
+        if not first:
+            hand_over(at)
+
+    def ring_step(n):
+        at = chunk(0, -n)
+        weight_copy(at, right, N_X).wait_recv()
+        if n < N_Z // 2:
+            weight_copy(at, right, N_X).start()
+        spread(at)
+        if n < N_Z // 2:
+            at = chunk(0, n)
+            weight_copy(at, left, N_X + 1).wait_recv()
+            if n < N_Z // 2 - 1:
+                weight_copy(at, left, N_X + 1).start()
+            spread(at)
+
+    def drain(n):
+        steps = [0] if n == 0 else [-n] if n == N_Z // 2 else [-n, n]
+        for dz in steps:
+            for i in range(N_X - 1):
+                at = chunk(i + 1, dz)
+                weight_copy(at, across[i], 1 + i).wait_recv()
+                hand_over(at)
 
     started = []
-    for i, peer in enumerate(PEERS):
-        device, rank = place(*peer)
-        started.append(
-            pltpu.make_async_remote_copy(
-                src_ref=meta_ref, dst_ref=meta_recv.at[me], send_sem=meta_send.at[i],
-                recv_sem=meta_sem.at[me], device_id=device, device_id_type=MESH,
-            )
-        )
-        started[-1].start()
-    for kind in (1, 0, 2):
-        for i, peer in enumerate(PEERS):
-            device, rank = place(*peer)
+
+    def issue(messages):
+        for kind, i in messages:
+            device, rank = place(*PEERS[i])
             started.append(
                 pltpu.make_async_remote_copy(
                     src_ref=proj_ref.at[:, :, columns(rank, kind)], dst_ref=recv[kind].at[pl.ds(2 * me, 2)],
@@ -80,6 +127,27 @@
                 )
             )
             started[-1].start()
+
+    weight_copy(dp, right, N_X, True).start()
+    weight_copy(dp, left, N_X + 1, True).start()
+    for i, peer in enumerate(PEERS):
+        device, rank = place(*peer)
+        started.append(
+            pltpu.make_async_remote_copy(
+                src_ref=meta_ref, dst_ref=meta_recv.at[me], send_sem=meta_send.at[i],
+                recv_sem=meta_sem.at[me], device_id=device, device_id_type=MESH,
+            )
+        )
+        started[-1].start()
+    messages = [(kind, i) for kind in (1, 0, 2) for i in range(len(PEERS))]
+    issue(messages[:FIRST])
+    spread(dp, True)
+    for n in range(1, EARLY + 1):
+        ring_step(n)
+        if n >= 2:
+            drain(n - 2)
+        issue(messages[FIRST + (n - 1) * BATCH : FIRST + n * BATCH])
+    issue(messages[FIRST + EARLY * BATCH :])
 
     def wait_kind(kind):
         for i, peer in enumerate(PEERS):
@@ -143,7 +211,15 @@
             probs[i, :, w * BLK : (w + 1) * BLK] = jnp.exp2((parts[w] - row_max) * EXP2_SCALE).astype(jnp.bfloat16)
         return carry
 
-    lax.fori_loop(0, 2 * PACK, score_step, 0)
+    jobs = [(n, n - 2) for n in range(EARLY + 1, N_Z // 2 + 1)]
+    jobs += [(None, N_Z // 2 - 1), (None, N_Z // 2)]
+    per = 2 * PACK // len(jobs)
+    for i, (n, m) in enumerate(jobs):
+        last = 2 * PACK if i == len(jobs) - 1 else (i + 1) * per
+        lax.fori_loop(i * per, last, score_step, 0)
+        if n is not None:
+            ring_step(n)
+        drain(m)
     wait_kind(2)
     gather(2, v_pack)
 
@@ -184,22 +260,49 @@
         copy.wait_recv()
     for copy in started:
         copy.wait_send()
-    finish = pltpu.make_async_copy(merged, out_ref, local_sem.at[4])
-    finish.start()
-    finish.wait()
+    own[4].wait()
+    pieces = N_X * N_Z - 1
+
+    def weight_bytes(count, sender, sem=None):
+        part = w_all.at[pl.ds(0, count), :, half]
+        return pltpu.make_async_remote_copy(
+            src_ref=part, dst_ref=part, send_sem=w_sends.at[sender],
+            recv_sem=w_sem.at[N_X * N_Z] if sem is None else sem, device_id=sibling, device_id_type=MESH,
+        )
+
+    weight_bytes(pieces, 0).wait_recv()
+
+    def project(n, carry):
+        at = pl.ds(pl.multiple_of(n * TILE, TILE), TILE)
+        tiles[n] = jnp.dot(
+            merged[...].reshape(2 * BLK, -1), w_all[:, :, at].reshape(-1, TILE), preferred_element_type=jnp.float32
+        ).astype(jnp.bfloat16)
+        pltpu.make_async_copy(tiles.at[n], out_ref.at[:, at], local_sem.at[6 + n]).start()
+        return carry
+
+    count = features // TILE
+    lax.fori_loop(0, count, project, 0)
+    for n in range(count):
+        pltpu.make_async_copy(tiles.at[n], out_ref.at[:, pl.ds(n * TILE, TILE)], local_sem.at[6 + n]).wait()
+    weight_bytes(pieces, 0).wait_send()
+    for i in range(1, N_X):
+        weight_bytes(N_Z, i).wait_send()
+    weight_bytes(N_Z // 2, N_X).wait_send()
+    weight_bytes(N_Z // 2 - 1, N_X + 1).wait_send()
 
 
 def body(projections, block_source, clip_ids, out_weight):
     rows, width = projections.shape
     heads = width // (3 * HEAD)
+    shard, features = out_weight.shape
     meta = jnp.concatenate([block_source.reshape(-1) % (2 * PACK), clip_ids.reshape(-1)])
     meta = jnp.pad(meta[None, :], ((0, 7), (0, 128 - meta.shape[0])))
     kinds = pltpu.SemaphoreType.DMA((3, GROUP))
     ranks = pltpu.SemaphoreType.DMA((GROUP,))
-    attended = pl.pallas_call(
+    return pl.pallas_call(
         kernel,
-        out_shape=jax.ShapeDtypeStruct((2, BLK, heads * HEAD), jnp.bfloat16),
-        in_specs=[pl.BlockSpec(memory_space=pl.ANY)] * 2,
+        out_shape=jax.ShapeDtypeStruct((rows, features), jnp.bfloat16),
+        in_specs=[pl.BlockSpec(memory_space=pl.ANY)] + [pl.BlockSpec(memory_space=pltpu.HBM)] * 2,
         out_specs=pl.BlockSpec(memory_space=pl.ANY),
         scratch_shapes=[
             pltpu.VMEM((2 * PACK, BLK, HEAD), jnp.bfloat16),
@@ -212,20 +315,18 @@
             pltpu.VMEM((2 * PACK, BLK, WIN * BLK), jnp.bfloat16),
             pltpu.VMEM((GROUP, 2, BLK, HEAD), jnp.bfloat16),
             pltpu.VMEM((2, BLK, heads * HEAD), jnp.bfloat16),
+            pltpu.VMEM((N_X * N_Z, shard, features), jnp.bfloat16),
+            pltpu.VMEM((features // TILE, rows, TILE), jnp.bfloat16),
             kinds, kinds, ranks, ranks, ranks, ranks,
-            pltpu.SemaphoreType.DMA((5,)),
+            pltpu.SemaphoreType.DMA((N_X * N_Z + 1,)),
+            pltpu.SemaphoreType.DMA((N_X + 2,)),
+            pltpu.SemaphoreType.DMA((6 + features // TILE,)),
         ],
         compiler_params=pltpu.CompilerParams(
-            collective_id=0, has_side_effects=True, vmem_limit_bytes=48 * 2**20
+            collective_id=0, has_side_effects=True, vmem_limit_bytes=63 * 2**20
         ),
         name="attend",
-    )(meta, projections.reshape(2, BLK, width))
-    result = jnp.dot(
-        attended.reshape(rows, heads * HEAD),
-        lax.all_gather(out_weight, "dp", axis=0, tiled=True),
-        preferred_element_type=jnp.float32,
-    )
-    return result.astype(jnp.bfloat16)
+    )(meta, projections.reshape(2, BLK, width), out_weight)
 
 
 def solution(mesh):

time: 178 us -> 90.6 us (0.51)
  the two profiles are of different devices: /device:TPU:32 before, /device:TPU:1 now
where the time goes in v2:
time: 90.6 us; the launch traced here: 90.5 us
  Pallas kernels  86.4 us (95%)
  local copies, waits for them, and re-layouts  2.66 us (3%)
  other arithmetic  1.39 us (2%)
    pallas_call x1, Pallas kernels, body(): pl.pallas_call(kernel, out_shape=jax.ShapeDtypeStruct((rows, features), j...  86.4 us
    unnamed x1, local copies, waits for them, and re-layouts  2.06 us

profile of v2, /device:TPU:1, one launch (start us, length us, event | category | flops | bytes accessed | tf_op | source)
XLA Modules:
  0.0 90.5 jit_solution(1384978072670710690)
XLA Ops:
  0.0 0.7 and_select_fusion
  0.7 0.7 add_bitcast_fusion
  1.4 0.6 pad.4.meta_ref
  2.0 86.4 %attend.1 = bf16[256,1536]{1,0:T(8,128)(2,1)} custom-call(s32[8,128]{1,0:T(8,128)} %pad.4.meta_ref, bf16[2,128,6144]{2,1,0:T(8,128)(2,1)} %bitcast.6, bf16[32,1536]{1,0:T(8,128)(2,1)} %w_ref.1), custom_call_target="tpu_custom_call" | custom-call | tf_op jit(solution)/shard_map/attend/pallas_call | solution.py:302
  88.4 2.1 %copy.6 = bf16[256,1536]{1,0:T(8,128)(2,1)} copy(bf16[256,1536]{1,0:T(8,128)(2,1)} %attend.1) | data formatting | bytes 1572864
